TPU v7x, 128 devices: a whole 4x4x4 slice. The times are simulated.
128 devices in a mesh: lm: 8 (over z, x_hi), sl: 16 (over y, x_lo, core).
Axes of the slice: x: 4 (x_hi: 2, x_lo: 2; x = x_hi * 2 + x_lo), y: 4, z: 4, core: 2. Of those that a mesh axis runs over, the one named last changes fastest.
Arguments:
- slab: bfloat16 [16384, 1024], P('sl'), may hold values from -6 to 6
- landmarks: bfloat16 [32768, 1024], P(('lm', 'sl')), may hold values from -6 to 6
- codes: bfloat16 [32768, 96], P(('lm', 'sl')), may hold values from -4 to 4
- exponents: int32 [256], P(('lm', 'sl')), may hold values from -3 to 3
- eigvec: bfloat16 [96, 64], replicated, may hold values from -0.625 to 0.625
- ritz: float32 [64], replicated, may hold values from 0.5 to 4
Outputs:
- extended: float32 [16384, 64], P('sl')
All inputs are finite; a program needn't handle non-finite values.
Results may differ from a plain program's by a relative error of at most 0.004.
Values may be sent and summed in bfloat16 or wider, within the bound.
A program may use at most 128 MiB of HBM per device.

v0:
```python
import math
import jax
import jax.numpy as jnp
from jax import lax
from jax.sharding import PartitionSpec as P

BLOCK = 128


def affinity_sum(rows, land_piece, vec_piece, coeff):
    scores = jnp.dot(rows, land_piece.T, preferred_element_type=jnp.float32) * coeff
    affinity = jnp.exp(scores).astype(jnp.bfloat16)
    return jnp.dot(affinity, vec_piece, preferred_element_type=jnp.float32)


def local(slab, landmarks, codes, exponents, eigvec, ritz):
    total_land = codes.shape[0] * lax.axis_size("lm") * lax.axis_size("sl")
    coeff = 1.0 / math.sqrt(slab.shape[1])
    factor = 1.0 / (ritz * math.sqrt(total_land))
    scale = jnp.exp2(exponents.astype(jnp.float32))
    rows_scale = jnp.repeat(scale, BLOCK)
    basis = (codes.astype(jnp.float32) * rows_scale[:, None]).astype(jnp.bfloat16)
    vectors = jnp.dot(basis, eigvec, preferred_element_type=jnp.float32).astype(jnp.bfloat16)
    terms = affinity_sum(lax.all_gather(slab, "sl", axis=0, tiled=True), landmarks, vectors, coeff)
    partial_sum = lax.psum_scatter(terms, "sl", scatter_dimension=0, tiled=True)
    summed = lax.psum(partial_sum, "lm")
    return summed * factor[None, :]


def solution(mesh):
    return jax.shard_map(
        local,
        mesh=mesh,
        in_specs=(
            P("sl", None),
            P(("lm", "sl"), None),
            P(("lm", "sl"), None),
            P(("lm", "sl")),
            P(),
            P(),
        ),
        out_specs=P("sl", None),
        check_vma=False,
    )
```

profile of v0, /device:TPU:0, one launch (start us, length us, event | category | flops | bytes accessed | tf_op | source)
XLA Modules:
  0.0 365.8 jit_solution(13882836581902991858)
XLA Ops:
  6.5 0.0 copy-start
  6.5 0.0 all-gather.2.cloned.1.call-start
  6.5 0.7 all-gather.2.cloned.1.call-update
  7.3 0.0 reduce-scatter.2.cloned.1.call-start
  7.3 0.7 multiply_exponential_fusion
  8.0 0.1 broadcast_bitcast_fusion
  8.0 1.0 convolution_convert_fusion
  9.0 0.0 copy-start.1
  9.0 173.1 %all-gather.2.cloned.1.call-done = bf16[16384,1024]{1,0:T(8,128)(2,1)} async-done(((bf16[1024,1024]{1,0:T(8,128)(2,1)}), bf16[16384,1024]{1,0:T(8,128)(2,1)}) %all-gather.2.cloned.1.call-update) | async-done | bytes 33554448 | tf_op jit(solution)/shard_map/all_gather | solution.py:24
  182.1 0.0 copy-done
  182.1 18.8 %fusion.2 = f32[16384,64]{0,1:T(8,128)} fusion(bf16[256,64]{1,0:T(8,128)(2,1)S(1)} %convolution_convert_fusion, bf16[16384,1024]{1,0:T(8,128)(2,1)} %all-gather.2.cloned.1.call-done, bf16[256,1024]{1,0:T(8,128)(2,1)S(1)} %copy-done), kind=kOutput, calls=%fused_computation.3 | convolution fusion | flops 9135194112 | bytes 38305792 | tf_op jit(solution)/shard_map/dot_general | solution.py:13
  201.0 0.0 reduce-scatter.2.cloned.1.call-update
  201.0 0.0 all-reduce.2.cloned.1.call-start
  201.1 70.5 %reduce-scatter.2.cloned.1.call-done = f32[1024,64]{0,1:T(8,128)} async-done(((f32[16384,64]{0,1:T(8,128)}), f32[1024,64]{0,1:T(8,128)}) %reduce-scatter.2.cloned.1.call-update) | async-done | bytes 262160 | tf_op jit(solution)/shard_map/reduce_scatter | solution.py:25
  271.5 0.0 all-reduce.2.cloned.1.call-update
  271.6 0.0 copy-done.1
  271.6 85.9 %all-reduce.2.cloned.1.call-done = f32[1024,64]{0,1:T(8,128)} async-done(((f32[1024,64]{0,1:T(8,128)}), f32[1024,64]{0,1:T(8,128)}) %all-reduce.2.cloned.1.call-update) | async-done | bytes 262160 | tf_op jit(solution)/shard_map/psum | solution.py:26
  357.5 1.7 broadcast_multiply_fusion
  (1 shorter events, 0.0 us)
Async XLA Ops:
  6.5 175.6 %copy-start = (bf16[256,1024]{1,0:T(8,128)(2,1)S(1)}, bf16[256,1024]{1,0:T(8,128)(2,1)}, u32[]{:S(2)}) copy-start(bf16[256,1024]{1,0:T(8,128)(2,1)} %param.7) | copy-start | bytes 1572868
  6.5 175.6 %all-gather.2.cloned.1.call-start = ((), (), s32[]{:S(2)}) async-start(), calls=%async_computation.1 | async-start | bytes 35651584 | tf_op jit(solution)/shard_map/all_gather | solution.py:24
  7.3 264.3 %reduce-scatter.2.cloned.1.call-start = ((), (), s32[]{:S(2)}) async-start(), calls=%async_computation.2 | async-start | bytes 4456448 | tf_op jit(solution)/shard_map/reduce_scatter | solution.py:25
  9.0 262.5 %copy-start.1 = (f32[64]{0:T(128)S(1)}, f32[64]{0:T(128)}, u32[]{:S(2)}) copy-start(f32[64]{0:T(128)} %param.11) | copy-start | bytes 772
  201.0 156.5 %all-reduce.2.cloned.1.call-start = ((), (), s32[]{:S(2)}) async-start(), calls=%async_computation.3 | async-start | bytes 524288 | tf_op jit(solution)/shard_map/psum | solution.py:26
Sparse Core Ops, SparseCore 0:
  9.1 173.0 all-gather.1
  201.1 70.3 reduce-scatter.1
  274.0 83.4 all-reduce.1
where the time goes:
time: 366 us
  waiting for transfers between devices  330 us (90%)
  matrix products  19.8 us (5%)
  between operations  13.1 us (4%)
    all_gather x1, waiting for transfers between devices, local(): lax.all_gather(slab, 'sl', axis=0, tiled=True)  173 us
    psum x1, waiting for transfers between devices, local(): summed = lax.psum(partial_sum, 'lm')  85.9 us
    reduce_scatter x1, waiting for transfers between devices, local(): partial_sum = lax.psum_scatter(terms, 'sl', scatter_dimension=0, tiled=True)  70.5 us
    dot_general x1, matrix products, affinity_sum(): return jnp.dot(affinity, vec_piece, preferred_element_type=jnp.float32)  18.8 us
  transfers between devices with their start and end apart: 3, of which 3 were waited for; matrix products, arithmetic and copies ran while one was open for 0% of the time, Pallas kernels for 0%

commit v1 on v0

--- a/solution.py
+++ b/solution.py
@@ -23,7 +23,7 @@
     vectors = jnp.dot(basis, eigvec, preferred_element_type=jnp.float32).astype(jnp.bfloat16)
     terms = affinity_sum(lax.all_gather(slab, "sl", axis=0, tiled=True), landmarks, vectors, coeff)
     partial_sum = lax.psum_scatter(terms, "sl", scatter_dimension=0, tiled=True)
-    summed = lax.psum(partial_sum, "lm")
+    summed = jnp.sum(lax.all_gather(partial_sum, "lm"), axis=0)
     return summed * factor[None, :]
 
 

time: 366 us -> 338 us (0.923)
  waiting for transfers between devices: 330 us -> 300 us
    psum x1 -> x0, waiting for transfers between devices: 85.9 us -> none  [local(): summed = lax.psum(partial_sum, 'lm')]
    all_gather x0 -> x1, waiting for transfers between devices: none -> 55.3 us  [local(): summed = jnp.sum(lax.all_gather(partial_sum, 'lm'), axis=0)]
  transfers between devices with their start and end apart: 3 -> 3, of which waited for: 3 -> 3; matrix products, arithmetic and copies ran while one was open for 0% -> 1% of each run, Pallas kernels for 0% -> 0%
where the time goes in v1:
time: 338 us; the launch traced here: 337 us
  waiting for transfers between devices  300 us (89%)
  matrix products  19.8 us (6%)
  between operations  13.1 us (4%)
    all_gather x1, waiting for transfers between devices, local(): lax.all_gather(slab, 'sl', axis=0, tiled=True)  173 us
    reduce_scatter x1, waiting for transfers between devices, local(): partial_sum = lax.psum_scatter(terms, 'sl', scatter_dimension=0, tiled=True)  70.5 us
    all_gather x1, waiting for transfers between devices, local(): summed = jnp.sum(lax.all_gather(partial_sum, 'lm'), axis=0)  55.3 us
    dot_general x1, matrix products, affinity_sum(): return jnp.dot(affinity, vec_piece, preferred_element_type=jnp.float32)  18.8 us
  transfers between devices with their start and end apart: 3, of which 3 were waited for; matrix products, arithmetic and copies ran while one was open for 1% of the time, Pallas kernels for 0%

profile of v1, /device:TPU:0, one launch (start us, length us, event | category | flops | bytes accessed | tf_op | source)
XLA Modules:
  0.0 337.5 jit_solution(5185767268095954319)
XLA Ops:
  6.5 0.0 copy-start
  6.5 0.0 all-gather.4.cloned.1.call-start
  6.5 0.7 all-gather.4.cloned.1.call-update
  7.3 0.0 reduce-scatter.2.cloned.1.call-start
  7.3 0.7 multiply_exponential_fusion
  8.0 0.1 broadcast_bitcast_fusion
  8.0 1.0 convolution_convert_fusion
  9.0 0.0 copy-start.1
  9.0 173.1 %all-gather.4.cloned.1.call-done = bf16[16384,1024]{1,0:T(8,128)(2,1)} async-done(((bf16[1024,1024]{1,0:T(8,128)(2,1)}), bf16[16384,1024]{1,0:T(8,128)(2,1)}) %all-gather.4.cloned.1.call-update) | async-done | bytes 33554448 | tf_op jit(solution)/shard_map/all_gather | solution.py:24
  182.1 0.0 copy-done
  182.1 18.8 %fusion.2 = f32[16384,64]{0,1:T(8,128)} fusion(bf16[256,64]{1,0:T(8,128)(2,1)S(1)} %convolution_convert_fusion, bf16[16384,1024]{1,0:T(8,128)(2,1)} %all-gather.4.cloned.1.call-done, bf16[256,1024]{1,0:T(8,128)(2,1)S(1)} %copy-done), kind=kOutput, calls=%fused_computation.3 | convolution fusion | flops 9135194112 | bytes 38305792 | tf_op jit(solution)/shard_map/dot_general | solution.py:13
  201.0 0.0 reduce-scatter.2.cloned.1.call-update
  201.0 0.0 all-gather.6.cloned.1.call-start
  201.1 70.5 %reduce-scatter.2.cloned.1.call-done = f32[1024,64]{0,1:T(8,128)} async-done(((f32[16384,64]{0,1:T(8,128)}), f32[1024,64]{0,1:T(8,128)}) %reduce-scatter.2.cloned.1.call-update) | async-done | bytes 262160 | tf_op jit(solution)/shard_map/reduce_scatter | solution.py:25
  271.5 0.0 all-gather.6.cloned.1.call-update
  271.6 0.0 copy-done.1
  271.6 55.3 %all-gather.6.cloned.1.call-done = f32[8192,64]{0,1:T(8,128)} async-done(((f32[1024,64]{0,1:T(8,128)}), f32[8192,64]{0,1:T(8,128)}) %all-gather.6.cloned.1.call-update) | async-done | bytes 2097168 | tf_op jit(solution)/shard_map/all_gather | solution.py:26
  326.9 2.8 copy.7
  329.6 0.5 bitcast_reduce_fusion
  330.2 0.8 broadcast_multiply_fusion
  (1 shorter events, 0.0 us)
Async XLA Ops:
  6.5 175.6 %copy-start = (bf16[256,1024]{1,0:T(8,128)(2,1)S(1)}, bf16[256,1024]{1,0:T(8,128)(2,1)}, u32[]{:S(2)}) copy-start(bf16[256,1024]{1,0:T(8,128)(2,1)} %param.7) | copy-start | bytes 1572868
  6.5 175.6 %all-gather.4.cloned.1.call-start = ((), (), s32[]{:S(2)}) async-start(), calls=%async_computation.1 | async-start | bytes 35651584 | tf_op jit(solution)/shard_map/all_gather | solution.py:24
  7.3 264.3 %reduce-scatter.2.cloned.1.call-start = ((), (), s32[]{:S(2)}) async-start(), calls=%async_computation.2 | async-start | bytes 4456448 | tf_op jit(solution)/shard_map/reduce_scatter | solution.py:25
  9.0 262.5 %copy-start.1 = (f32[64]{0:T(128)S(1)}, f32[64]{0:T(128)}, u32[]{:S(2)}) copy-start(f32[64]{0:T(128)} %param.11) | copy-start | bytes 772
  201.0 125.8 %all-gather.6.cloned.1.call-start = ((), (), s32[]{:S(2)}) async-start(), calls=%async_computation.3 | async-start | bytes 2359296 | tf_op jit(solution)/shard_map/all_gather | solution.py:26
Sparse Core Ops, SparseCore 0:
  9.1 173.0 all-gather.3
  201.1 70.3 reduce-scatter.1
  273.8 52.9 all-gather.5

commit v2 on v0

--- a/solution.py
+++ b/solution.py
@@ -21,7 +21,14 @@
     rows_scale = jnp.repeat(scale, BLOCK)
     basis = (codes.astype(jnp.float32) * rows_scale[:, None]).astype(jnp.bfloat16)
     vectors = jnp.dot(basis, eigvec, preferred_element_type=jnp.float32).astype(jnp.bfloat16)
-    terms = affinity_sum(lax.all_gather(slab, "sl", axis=0, tiled=True), landmarks, vectors, coeff)
+    terms = affinity_sum(
+        jnp.concatenate(
+            lax.all_to_all(jnp.stack([slab] * lax.axis_size("sl")), "sl", 0, 0), axis=0
+        ),
+        landmarks,
+        vectors,
+        coeff,
+    )
     partial_sum = lax.psum_scatter(terms, "sl", scatter_dimension=0, tiled=True)
     summed = lax.psum(partial_sum, "lm")
     return summed * factor[None, :]

time: 366 us -> 574 us (1.57)
  waiting for transfers between devices: 330 us -> 521 us
  local copies, waits for them, and re-layouts: 0.08 us -> 12.3 us
  starting transfers between devices: 0.08 us -> 6.18 us
    all_to_all x0 -> x1, waiting for transfers between devices: none -> 365 us  [local(): lax.all_to_all(jnp.stack([slab] * lax.axis_size('sl')), 'sl', 0, 0)]
    all_gather x1 -> x0, waiting for transfers between devices: 173 us -> none  [local(): lax.all_gather(slab, 'sl', axis=0, tiled=True)]
    another operation x0 -> x1, local copies, waits for them, and re-layouts: none -> 12.2 us  [local(): jnp.stack([slab] * lax.axis_size('sl'))]
    all_to_all x0 -> x1, starting transfers between devices: none -> 6.09 us  [local(): lax.all_to_all(jnp.stack([slab] * lax.axis_size('sl')), 'sl', 0, 0)]
where the time goes in v2:
time: 574 us
  waiting for transfers between devices  521 us (91%)
  matrix products  19.1 us (3%)
  between operations  13.5 us (2%)
  local copies, waits for them, and re-layouts  12.3 us (2%)
  starting transfers between devices  6.18 us (1%)
    all_to_all x1, waiting for transfers between devices, local(): lax.all_to_all(jnp.stack([slab] * lax.axis_size('sl')), 'sl', 0, 0)  365 us
    psum x1, waiting for transfers between devices, local(): summed = lax.psum(partial_sum, 'lm')  86.2 us
    reduce_scatter x1, waiting for transfers between devices, local(): partial_sum = lax.psum_scatter(terms, 'sl', scatter_dimension=0, tiled=True)  70.2 us
    dot_general x1, matrix products, affinity_sum(): return jnp.dot(affinity, vec_piece, preferred_element_type=jnp.float32)  18.9 us
    another operation x1, local copies, waits for them, and re-layouts, local(): jnp.stack([slab] * lax.axis_size('sl'))  12.2 us
  transfers between devices with their start and end apart: 3, of which 3 were waited for; matrix products, arithmetic and copies ran while one was open for 0% of the time, Pallas kernels for 0%

profile of v2, /device:TPU:0, one launch (start us, length us, event | category | flops | bytes accessed | tf_op | source)
XLA Modules:
  0.0 573.8 jit_solution(6835796730593689424)
XLA Ops:
  6.5 0.0 copy-start
  6.5 12.2 %stack.2 = bf16[16,1024,1024]{2,1,0:T(8,128)(2,1)} broadcast(bf16[1024,1024]{1,0:T(8,128)(2,1)} %param.6), dimensions={1,2} | broadcast | bytes 35651584 | tf_op jit(solution)/shard_map/stack | solution.py:26
  18.8 0.0 copy-start.3
  18.8 0.0 copy-start.1
  18.8 0.0 copy-start.2
  18.8 6.1 %all-to-all-start = ((bf16[16,1024,1024]{2,1,0:T(8,128)(2,1)}), bf16[16,1024,1024]{2,1,0:T(8,128)(2,1)}, u32[]{:S(2)}, u32[]{:S(2)}) async-start(bf16[16,1024,1024]{2,1,0:T(8,128)(2,1)} %stack.2), calls=%async_computation | async-start | bytes 67108864 | tf_op jit(solution)/shard_map/all_to_all | solution.py:26
  24.9 0.0 reduce-scatter.2.cloned.1.call-start
  24.9 0.0 copy-done.3
  25.0 0.1 broadcast_bitcast_fusion
  25.0 0.0 copy-done.1
  25.0 0.0 copy-done.2
  25.0 0.2 convolution_convert_fusion
  25.2 364.6 %all-to-all-done = bf16[16,1024,1024]{2,1,0:T(8,128)(2,1)} async-done(((bf16[16,1024,1024]{2,1,0:T(8,128)(2,1)}), bf16[16,1024,1024]{2,1,0:T(8,128)(2,1)}, u32[]{:S(2)}, u32[]{:S(2)}) %all-to-all-start) | async-done | bytes 33554464 | tf_op jit(solution)/shard_map/all_to_all | solution.py:26
  389.9 0.0 copy-done
  389.9 0.0 copy-start.4
  389.9 18.9 %fusion.2 = f32[16384,64]{0,1:T(8,128)} fusion(bf16[256,64]{1,0:T(8,128)(2,1)S(1)} %convolution_convert_fusion, bf16[16384,1024]{1,0:T(8,128)(2,1)} %bitcast, bf16[256,1024]{1,0:T(8,128)(2,1)S(1)} %copy-done), kind=kOutput, calls=%fused_computation.3 | convolution fusion | flops 9135194112 | bytes 38305792 | tf_op jit(solution)/shard_map/dot_general | solution.py:13
  408.7 0.0 reduce-scatter.2.cloned.1.call-update
  408.8 0.0 all-reduce.2.cloned.1.call-start
  408.8 70.2 %reduce-scatter.2.cloned.1.call-done = f32[1024,64]{0,1:T(8,128)} async-done(((f32[16384,64]{0,1:T(8,128)}), f32[1024,64]{0,1:T(8,128)}) %reduce-scatter.2.cloned.1.call-update) | async-done | bytes 262160 | tf_op jit(solution)/shard_map/reduce_scatter | solution.py:32
  479.0 0.0 all-reduce.2.cloned.1.call-update
  479.0 0.0 copy-done.4
  479.1 86.2 %all-reduce.2.cloned.1.call-done = f32[1024,64]{0,1:T(8,128)} async-done(((f32[1024,64]{0,1:T(8,128)}), f32[1024,64]{0,1:T(8,128)}) %all-reduce.2.cloned.1.call-update) | async-done | bytes 262160 | tf_op jit(solution)/shard_map/psum | solution.py:33
  565.2 1.7 broadcast_multiply_fusion
  (2 shorter events, 0.0 us)
Async XLA Ops:
  6.5 383.3 %copy-start = (bf16[256,1024]{1,0:T(8,128)(2,1)S(1)}, bf16[256,1024]{1,0:T(8,128)(2,1)}, u32[]{:S(2)}) copy-start(bf16[256,1024]{1,0:T(8,128)(2,1)} %param.7) | copy-start | bytes 1572868
  18.8 6.2 %copy-start.3 = (s32[2]{0:T(128)S(1)}, s32[2]{0:T(128)}, u32[]{:S(2)}) copy-start(s32[2]{0:T(128)} %param.9) | copy-start | bytes 28
  18.8 6.3 %copy-start.1 = (bf16[256,96]{0,1:T(8,128)(2,1)S(1)}, bf16[256,96]{0,1:T(8,128)(2,1)}, u32[]{:S(2)}) copy-start(bf16[256,96]{0,1:T(8,128)(2,1)} %param.8) | copy-start | bytes 147460
  18.8 6.3 %copy-start.2 = (bf16[96,64]{0,1:T(8,128)(2,1)S(1)}, bf16[96,64]{0,1:T(8,128)(2,1)}, u32[]{:S(2)}) copy-start(bf16[96,64]{0,1:T(8,128)(2,1)} %param.10) | copy-start | bytes 36868
  18.8 371.1 %all-to-all-start = ((bf16[16,1024,1024]{2,1,0:T(8,128)(2,1)}), bf16[16,1024,1024]{2,1,0:T(8,128)(2,1)}, u32[]{:S(2)}, u32[]{:S(2)}) async-start(bf16[16,1024,1024]{2,1,0:T(8,128)(2,1)} %stack.2), calls=%async_computation | async-start | bytes 67108864 | tf_op jit(solution)/shard_map/all_to_all | solution.py:26
  24.9 454.1 %reduce-scatter.2.cloned.1.call-start = ((), (), s32[]{:S(2)}) async-start(), calls=%async_computation.2 | async-start | bytes 4456448 | tf_op jit(solution)/shard_map/reduce_scatter | solution.py:32
  389.9 89.2 %copy-start.4 = (f32[64]{0:T(128)S(1)}, f32[64]{0:T(128)}, u32[]{:S(2)}) copy-start(f32[64]{0:T(128)} %param.11) | copy-start | bytes 772
  408.8 156.5 %all-reduce.2.cloned.1.call-start = ((), (), s32[]{:S(2)}) async-start(), calls=%async_computation.3 | async-start | bytes 524288 | tf_op jit(solution)/shard_map/psum | solution.py:33
Sparse Core Ops, SparseCore 0:
  408.9 70.0 reduce-scatter.1
  481.5 83.7 all-reduce.1
